TPU v7x, 128 devices: a whole 4x4x4 slice. The times are simulated.
128 devices in a mesh: space: 16 (over z, y_hi, core), tm: 8 (over y_lo, x).
Axes of the slice: x: 4, y: 4 (y_hi: 2, y_lo: 2; y = y_hi * 2 + y_lo), z: 4, core: 2. Of those that a mesh axis runs over, the one named last changes fastest.
Arguments:
- series: bfloat16 [32, 16384, 1024], P(None, 'space', 'tm'), may hold values from -1000 to 1000, as said below
Outputs:
- cross: float32 [512, 2048], P(('space', 'tm'))
Inputs may be any that keep to these rules, and one draw needn't show every extreme that they name: `series`: finite pressure samples.
All inputs are finite; a program needn't handle non-finite values.
Results may differ from a plain program's by a relative error of at most 0.0003.
Values may be sent and summed in bfloat16 or wider, within the bound.
A program may use at most 192 MiB of HBM per device.

v0:
```python
import math

import jax
import jax.numpy as jnp
from jax import lax
from jax.sharding import PartitionSpec as P


def cross_terms(shaped, norm_factor):
    gram_all = jnp.einsum(
        "ipcf,jpdf->fcdij",
        shaped,
        shaped,
        precision=lax.Precision.HIGHEST,
        preferred_element_type=jnp.float32,
    )
    real_sum = gram_all[:, 0, 0] + gram_all[:, 1, 1]
    imag_sum = gram_all[:, 1, 0] - gram_all[:, 0, 1]
    freq_local = shaped.shape[3]
    members = shaped.shape[0]
    return (
        jnp.stack([real_sum, imag_sum], axis=1).reshape(freq_local, 2 * members * members)
        * norm_factor
    )


def shards(series):
    members, pts_dev, frames_dev = series.shape
    space_count = lax.axis_size("space")
    time_count = lax.axis_size("tm")
    frames = frames_dev * time_count
    nfreq = frames // 2
    pts_group = pts_dev // time_count
    row_index = jnp.arange(nfreq, dtype=jnp.int32)
    time_index = jnp.arange(frames, dtype=jnp.int32)
    phase_int = row_index[:, None] * time_index[None, :] % frames
    angle = phase_int.astype(jnp.float32) * (2.0 * math.pi / frames)
    full_table = jnp.concatenate([jnp.cos(angle), -jnp.sin(angle)], axis=0)
    window = 0.5 - 0.5 * jnp.cos(2.0 * math.pi * time_index.astype(jnp.float32) / frames)
    norm_factor = 1.0 / (0.375 * frames * pts_dev * space_count)
    values = lax.all_to_all(series, "tm", split_axis=1, concat_axis=2, tiled=True).astype(
        jnp.float32
    )
    time_mean = jnp.mean(values, axis=2, keepdims=True)
    fluctuation = (values - time_mean) * window
    spectra = jnp.einsum(
        "mpt,jt->mpj",
        fluctuation,
        full_table,
        precision=lax.Precision.HIGHEST,
        preferred_element_type=jnp.float32,
    )
    shaped = spectra.reshape(spectra.shape[0], pts_group, 2, nfreq)
    partial_cross = cross_terms(shaped, norm_factor)
    return lax.psum_scatter(partial_cross, ("space", "tm"), scatter_dimension=0, tiled=True)


def solution(mesh):
    placed = (P(None, "space", "tm"),)
    return jax.shard_map(
        shards, mesh=mesh, in_specs=placed, out_specs=P(("space", "tm"), None), check_vma=False
    )
```

profile of v0, /device:TPU:32, one launch (start us, length us, event | category | flops | bytes accessed | tf_op | source)
XLA Modules:
  0.0 631.4 jit_solution(7391656282645276449)
XLA Ops:
  6.5 12.0 %copy.16 = bf16[32,1024,128]{2,0,1:T(8,128)(2,1)} copy(bf16[32,1024,128]{2,1,0:T(8,128)(2,1)} %param.1) | data formatting | bytes 16777216 | tf_op args[0]
  18.5 5.3 all-to-all-start
  23.8 0.2 all-reduce.3.cloned.1.call-start
  24.1 8.2 %sine_negate_fusion = (f32[512,1024]{1,0:T(8,128)S(1)}, f32[512,1024]{1,0:T(8,128)S(1)}) fusion(), kind=kLoop, calls=%fused_computation.18 | loop fusion | flops 7864320 | bytes 4194304 | tf_op jit(solution)/shard_map/neg | solution.py:38
  32.3 2.6 pad_maximum_fusion
  34.9 83.4 %all-to-all-done = bf16[32,1024,128]{2,0,1:T(8,128)(2,1)} async-done(((bf16[32,1024,128]{2,0,1:T(8,128)(2,1)}), bf16[32,1024,128]{2,0,1:T(8,128)(2,1)}, u32[]{:S(2)}, u32[]{:S(2)}) %all-to-all-start) | async-done | bytes 8388640 | tf_op jit(solution)/shard_map/all_to_all | solution.py:41
  118.3 9.8 %copy.17 = bf16[32,1024,128]{2,1,0:T(8,128)(2,1)} copy(bf16[32,1024,128]{2,0,1:T(8,128)(2,1)} %all-to-all-done) | data formatting | bytes 16777216 | tf_op jit(solution)/shard_map/all_to_all | solution.py:41
  128.1 4.6 fusion.1
  132.7 10.5 %fusion.2 = f32[32,128,8,128]{3,1,2,0:T(8,128)} fusion(f32[8,128]{1,0:T(8,128)S(1)} %multiply_subtract_fusion, f32[32,128]{1,0:T(8,128)S(1)} %broadcast_multiply_fusion, bf16[32,1024,128]{2,0,1:T(8,128)(2,1)} %all-to-all-done), kind=kLoop, calls=%fused_computation.3 | loop fusion | flops 12582912 | bytes 25186304 | tf_op jit(solution)/shard_map/mul | solution.py:45
  143.2 17.5 %copy.18 = f32[32,128,8,128]{1,3,2,0:T(8,128)} copy(f32[32,128,8,128]{3,1,2,0:T(8,128)} %fusion.2) | data formatting | bytes 33554432 | tf_op jit(solution)/shard_map/mul | solution.py:45
  160.7 110.8 %convolution_bitcast_fusion.1 = f32[32,128,2,512,1]{3,1,2,0,4:T(8,128)} fusion(f32[32,128,1024,1]{1,2,3,0:T(8,128)} %bitcast.36, f32[2,512,1024,1]{2,1,0,3:T(8,128)} %bitcast.38), kind=kOutput, calls=%fused_computation.5 | convolution fusion | flops 51539607552 | bytes 37748736 | tf_op jit(solution)/shard_map/mpt,jt->mpj/dot_general | solution.py:46
  271.5 20.2 %copy.26 = f32[32,128,2,512,1]{1,0,4,2,3:T(8,128)} copy(f32[32,128,2,512,1]{3,1,2,0,4:T(8,128)} %convolution_bitcast_fusion.1) | data formatting | bytes 33554432 | tf_op jit(solution)/shard_map/mpt,jt->mpj/dot_general | solution.py:46
  291.7 20.2 %copy.27 = f32[32,128,2,512,1]{1,0,2,4,3:T(8,128)} copy(f32[32,128,2,512,1]{3,1,2,0,4:T(8,128)} %convolution_bitcast_fusion.1) | data formatting | bytes 33554432 | tf_op jit(solution)/shard_map/mpt,jt->mpj/dot_general | solution.py:46
  312.0 88.6 %convolution_bitcast_fusion = f32[512,2,2,32,32]{3,4,1,2,0:T(8,128)} fusion(f32[32,128,2,512,1]{1,0,4,2,3:T(8,128)} %copy.26, f32[32,128,2,512,1]{1,0,2,4,3:T(8,128)} %copy.27), kind=kOutput, calls=%fused_computation.4 | convolution fusion | flops 3221225472 | bytes 41943040 | tf_op jit(solution)/shard_map/ipcf,jpdf->fcdij/dot_general | solution.py:10
  400.6 19.0 %fusion.4 = (f32[512,1,32,32]{2,3,0,1:T(8,128)}, f32[512,1,32,32]{2,3,0,1:T(8,128)}) fusion(f32[512,2,2,32,32]{3,4,1,2,0:T(8,128)} %convolution_bitcast_fusion), kind=kLoop, calls=%fused_computation.9 | loop fusion | flops 1048576 | bytes 12582912 | tf_op jit(solution)/shard_map/add | solution.py:17
  419.6 5.8 copy.22
  425.4 6.6 %copy.23 = f32[512,1,32,32]{0,3,2,1:T(8,128)} copy(f32[512,1,32,32]{2,3,0,1:T(8,128)} %get-tuple-element.6) | data formatting | bytes 4194304 | tf_op jit(solution)/shard_map/sub | solution.py:18
  432.0 4.3 maximum_multiply_fusion
  436.2 0.0 all-reduce.3.cloned.1.call-update
  436.3 185.6 %all-reduce.3.cloned.1.call-done = f32[512,2048]{0,1:T(8,128)} async-done(((f32[512,2048]{0,1:T(8,128)}), f32[512,2048]{0,1:T(8,128)}) %all-reduce.3.cloned.1.call-update) | async-done | bytes 4194320
  621.9 1.6 constant_dynamic-slice_fusion
  623.4 0.9 copy.24
  (2 shorter events, 0.1 us)
Async XLA Ops:
  18.5 99.8 %all-to-all-start = ((bf16[32,1024,128]{2,0,1:T(8,128)(2,1)}), bf16[32,1024,128]{2,0,1:T(8,128)(2,1)}, u32[]{:S(2)}, u32[]{:S(2)}) async-start(bf16[32,1024,128]{2,0,1:T(8,128)(2,1)} %copy.16), calls=%async_computation | async-start | bytes 16777216 | tf_op jit(solution)/shard_map/all_to_all | solution.py:41
  23.8 598.0 %all-reduce.3.cloned.1.call-start = ((), (), s32[]{:S(2)}) async-start(), calls=%async_computation.1 | async-start | bytes 8388608
Sparse Core Ops, SparseCore 0:
  436.4 185.4 all-reduce.2
where the time goes:
time: 639 us; the launch traced here: 631 us
  waiting for transfers between devices  269 us (42%)
  matrix products  199 us (31%)
  local copies, waits for them, and re-layouts  94.6 us (15%)
  other arithmetic  49.2 us (8%)
  between operations  13.7 us (2%)
    unnamed x2, waiting for transfers between devices  186 us
    dot_general x1, matrix products, shards(): jnp.einsum('mpt,jt->mpj', fluctuation, full_table, precision=lax.Precisio...  111 us
    dot_general x1, matrix products, cross_terms(): jnp.einsum('ipcf,jpdf->fcdij', shaped, shaped, precision=lax.Precision.HI...  88.6 us
    all_to_all x1, waiting for transfers between devices, shards(): lax.all_to_all(series, 'tm', split_axis=1, concat_axis=2, tiled=True)  83.4 us
    dot_general x2, local copies, waits for them, and re-layouts, shards(): jnp.einsum('mpt,jt->mpj', fluctuation, full_table, precision=lax.Precisio...  40.5 us
    add x1, other arithmetic, cross_terms(): real_sum = gram_all[:, 0, 0] + gram_all[:, 1, 1]  19 us
    mul x1, local copies, waits for them, and re-layouts, shards(): fluctuation = (values - time_mean) * window  17.5 us
    unnamed x2, local copies, waits for them, and re-layouts  13.5 us
  transfers between devices with their start and end apart: 2, of which 2 were waited for; matrix products, arithmetic and copies ran while one was open for 2% of the time, Pallas kernels for 0%

commit v1 on v0

v1 whole, which is shorter than its diff:
```python
import functools
import math

import jax
import jax.numpy as jnp
import ml_dtypes
import numpy as np
from jax import lax
from jax.experimental import pallas as pl
from jax.experimental.pallas import tpu as pltpu
from jax.sharding import PartitionSpec as P

MESH = pl.DeviceIdType.MESH
NT_DIMS = (((1,), (1,)), ((), ()))
CHUNKS = 8
FBLOCK = 128
TM_PEERS = ((1, 0), (2, 1), (3, 0), (0, 1), (1, 1), (2, 0), (3, 1))


def dft_table(frames):
    nfreq = frames // 2
    t = np.arange(frames)
    angle = 2.0 * np.pi * (np.arange(nfreq)[:, None] * t[None, :] % frames) / frames
    window = 0.5 - 0.5 * np.cos(2.0 * np.pi * t / frames)
    table = np.stack([np.cos(angle), -np.sin(angle)]) * window
    table = table - table.sum(axis=2, keepdims=True) / frames
    table[np.abs(table) < 1e-13] = 0.0
    bf16 = ml_dtypes.bfloat16
    high = table.astype(np.float32).astype(bf16)
    low = (table - high.astype(np.float64)).astype(np.float32).astype(bf16)
    high = high.reshape(2 * nfreq, frames)
    low = low.reshape(2 * nfreq, frames)
    order = np.argsort(np.abs(low.astype(np.float64)), axis=1)
    for first, count in ((0, 32), (32, 4), (36, 1), (37, 1)):
        rest = (high.astype(np.float64) + low.astype(np.float64)).sum(axis=1, keepdims=True)
        cols = order[:, first : first + count]
        rows = np.arange(2 * nfreq)[:, None]
        low[rows, cols] = (low[rows, cols].astype(np.float64) - rest / count).astype(np.float32).astype(bf16)
    parts = np.stack([high, low]).reshape(2, 2, nfreq // FBLOCK, FBLOCK, frames)
    return parts.transpose(2, 0, 1, 3, 4).reshape(nfreq // FBLOCK, 2, 2 * FBLOCK, frames)


def split(value):
    high = value.astype(jnp.bfloat16)
    return high, (value - high.astype(jnp.float32)).astype(jnp.bfloat16)


def matmul_nt(a, b):
    return lax.dot_general(a, b, NT_DIMS, preferred_element_type=jnp.float32)


def kernel(
    norm, x_ref, table_ref, o_ref,
    recv, table, xre, xim, part_z, part_p, core_z, core_p, got_z, got_zp, got_p, got_pz,
    local_sem, table_sem, a2a_send, a2a_recv, core_send, core_recv, z_send, z_recv, p_send, p_recv,
):
    space, tm = lax.axis_index("space"), lax.axis_index("tm")
    core, y_hi, z = space % 2, space // 2 % 2, space // 4
    x, y_lo = tm % 4, tm // 4
    members, block = recv.shape[1], recv.shape[2]
    per_chunk = members // CHUNKS
    nfreq = xre.shape[0] // members
    plane = y_hi * 8 + y_lo * 4 + x

    def tm_peer(r):
        dx, dy = TM_PEERS[r]
        return (y_lo + dy) % 2 * 4 + (x + dx) % 4

    def tm_source(r):
        dx, dy = TM_PEERS[r]
        return (y_lo + 2 - dy) % 2 * 4 + (x + 4 - dx) % 4

    def device(z, plane, core):
        return z * 4 + plane // 8 * 2 + core, plane % 8

    def plane_peer(d):
        dyh, dyl, dx = d // 8, d // 4 % 2, d % 4
        ahead = (y_hi + dyh) % 2 * 8 + (y_lo + dyl) % 2 * 4 + (x + dx) % 4
        return ahead

    barrier = pltpu.get_barrier_semaphore()
    greeted = [device(z, plane_peer(d), core) for d in range(1, 16)]
    greeted += [device((z + d) % 4, plane, core) for d in range(1, 4)]
    greeted += [device(z, plane, 1 - core)]
    for peer in greeted:
        pl.semaphore_signal(barrier, inc=1, device_id=peer, device_id_type=MESH)
    pl.semaphore_wait(barrier, len(greeted))

    def snapshots(c, r):
        peer = tm_peer(r)
        return pltpu.make_async_remote_copy(
            src_ref=x_ref.at[pl.ds(c * per_chunk, per_chunk), pl.ds(peer * block, block), :],
            dst_ref=recv.at[tm, pl.ds(c * per_chunk, per_chunk)],
            send_sem=a2a_send.at[c, r],
            recv_sem=a2a_recv.at[c, r],
            device_id=(space, peer),
            device_id_type=MESH,
        )

    @pl.loop(0, CHUNKS)
    def _(c):
        for r in range(len(TM_PEERS)):
            snapshots(c, r).start()

    table_copy = pltpu.make_async_copy(table_ref, table, table_sem)
    table_copy.start()
    own_copy = pltpu.make_async_copy(x_ref.at[:, pl.ds(tm * block, block), :], recv.at[tm], local_sem)
    own_copy.start()
    table_copy.wait()
    own_copy.wait()

    @pl.loop(0, CHUNKS)
    def _(c):
        for r in range(len(TM_PEERS)):
            snapshots(c, r).wait_recv()
        first = c * per_chunk

        @pl.loop(0, nfreq // FBLOCK)
        def _(b):
            samples = jnp.concatenate(
                [recv[k, pl.ds(first, per_chunk)].reshape(per_chunk * block, block) for k in range(8)], axis=1
            )
            spectra = matmul_nt(table[b, 0], samples) + matmul_nt(table[b, 1], samples)
            for m in range(per_chunk):
                rows = pl.ds(b * (FBLOCK * members) + first + m, FBLOCK, stride=members)
                columns = slice(m * block, (m + 1) * block)
                xre[rows, :] = spectra[:FBLOCK, columns]
                xim[rows, :] = spectra[FBLOCK:, columns]

    lane = lax.broadcasted_iota(jnp.int32, (members, 4 * members), 1)
    row = lax.broadcasted_iota(jnp.int32, (members, 4 * members), 0)
    lane_f, lane_j = lane // members, lane % members
    half = members // 2

    def pick(tile):
        out = tile[3 * members :]
        for f in range(3):
            out = jnp.where(lane_f == f, tile[f * members : (f + 1) * members], out)
        return out

    def cross(zz, pp, cc):
        sp, t = device(zz, pp, cc)
        rows = pl.ds((sp * 8 + t) * (4 * members), 4 * members)
        re_hi, re_lo = split(xre[rows, :])
        im_hi, im_lo = split(xim[rows, :])
        a_hi = jnp.concatenate([re_hi, im_hi], axis=1)
        a_lo = jnp.concatenate([re_lo, im_lo], axis=1)
        b_hi = jnp.concatenate([a_hi, jnp.concatenate([-im_hi, re_hi], axis=1)], axis=0)
        b_lo = jnp.concatenate([a_lo, jnp.concatenate([-im_lo, re_lo], axis=1)], axis=0)
        gram = matmul_nt(a_hi, b_hi) + matmul_nt(a_lo, b_hi) + matmul_nt(a_hi, b_lo)
        return jnp.where(row >= lane_j, pick(gram[:, : 4 * members]), pick(gram[:, 4 * members :]))

    other = 1 - core

    @pl.loop(0, 64)
    def _(n):
        zz, pp = n // 16, n % 16
        tile = cross(zz, pp, other)
        part_z[0, zz, pp] = tile[:half]
        part_p[0, pp, zz] = tile[half:]

    def to_core(k):
        return pltpu.make_async_remote_copy(
            src_ref=(part_z, part_p)[k].at[0],
            dst_ref=(core_z, core_p)[k],
            send_sem=core_send.at[k],
            recv_sem=core_recv.at[k],
            device_id=(space + 1 - 2 * core, tm),
            device_id_type=MESH,
        )

    for k in range(2):
        to_core(k).start()

    @pl.loop(0, 64)
    def _(n):
        zz, pp = n // 16, n % 16
        tile = cross(zz, pp, core)
        part_z[1, zz, pp] = tile[:half]
        part_p[1, pp, zz] = tile[half:]

    for k in range(2):
        to_core(k).wait_recv()
    part_z[1] += core_z[...]
    part_p[1] += core_p[...]

    def over_z(stage, d):
        zz = (z + d) % 4
        src, dst = ((part_z.at[1, zz], got_z.at[d]), (part_p.at[1, plane, zz], got_pz.at[d]))[stage]
        return pltpu.make_async_remote_copy(
            src_ref=src,
            dst_ref=dst,
            send_sem=z_send.at[stage, d],
            recv_sem=z_recv.at[stage, d],
            device_id=device(zz, plane, core),
            device_id_type=MESH,
        )

    def over_plane(stage, d):
        pp = plane_peer(d)
        src, dst = ((part_p.at[1, pp], got_p.at[d]), (part_z.at[1, z, pp], got_zp.at[d]))[stage]
        return pltpu.make_async_remote_copy(
            src_ref=src,
            dst_ref=dst,
            send_sem=p_send.at[stage, d],
            recv_sem=p_recv.at[stage, d],
            device_id=device(z, pp, core),
            device_id_type=MESH,
        )

    for d in range(1, 4):
        over_z(0, d).start()
    for d in range(1, 16):
        over_plane(0, d).start()
    for d in range(1, 4):
        over_z(0, d).wait_recv()
    total = part_z[1, z]
    for d in range(1, 4):
        total = total + got_z[d]
    part_z[1, z] = total
    for d in range(1, 16):
        over_plane(1, d).start()
    for d in range(1, 16):
        over_plane(0, d).wait_recv()
    total = part_p[1, plane]
    for d in range(1, 16):
        total = total + got_p[d]
    part_p[1, plane] = total
    for d in range(1, 4):
        over_z(1, d).start()
    for d in range(1, 16):
        over_plane(1, d).wait_recv()
    upper = part_z[1, z, plane]
    for d in range(1, 16):
        upper = upper + got_zp[d]
    for d in range(1, 4):
        over_z(1, d).wait_recv()
    lower = part_p[1, plane, z]
    for d in range(1, 4):
        lower = lower + got_pz[d]

    mixed = jnp.concatenate([upper, lower], axis=0) * norm
    spread = jnp.concatenate([jnp.where(lane_f == f, mixed, 0.0) for f in range(4)], axis=0).T
    turned = spread[:members]
    for f in range(1, 4):
        turned = turned + spread[f * members : (f + 1) * members]
    real = jnp.where(row >= lane_j, mixed, turned)
    imag = jnp.where(row < lane_j, mixed, jnp.where(row == lane_j, 0.0, -turned))
    for part, value in enumerate((real, imag)):
        for bit in (2, 1):
            row_bit, lane_bit = row // bit % 2, lane_f // bit % 2
            up = pltpu.roll(pltpu.roll(value, bit * members, 1), members - bit, 0)
            down = pltpu.roll(pltpu.roll(value, (4 - bit) * members, 1), bit, 0)
            value = jnp.where(row_bit == lane_bit, value, jnp.where(row_bit == 0, up, down))
        for u in range(members // 4):
            start = (part * members // 4 + u) * 4 * members
            o_ref[:, start : start + 4 * members] = value[4 * u : 4 * u + 4]

    @pl.loop(0, CHUNKS)
    def _(c):
        for r in range(len(TM_PEERS)):
            snapshots(c, r).wait_send()

    for k in range(2):
        to_core(k).wait_send()
    for stage in range(2):
        for d in range(1, 4):
            over_z(stage, d).wait_send()
        for d in range(1, 16):
            over_plane(stage, d).wait_send()


def shards(series):
    members, pts_dev, frames_dev = series.shape
    space_count, time_count = lax.axis_size("space"), lax.axis_size("tm")
    frames, block = frames_dev * time_count, pts_dev // time_count
    nfreq, half = frames // 2, members // 2
    norm = 1.0 / (0.375 * frames * pts_dev * space_count)
    table = dft_table(frames)
    f32, bf16 = jnp.float32, jnp.bfloat16
    width = 4 * members
    dma = pltpu.SemaphoreType.DMA
    return pl.pallas_call(
        functools.partial(kernel, norm),
        out_shape=jax.ShapeDtypeStruct((nfreq // (space_count * time_count), 2 * members * members), f32),
        in_specs=[pl.BlockSpec(memory_space=pl.ANY)] * 2,
        out_specs=pl.BlockSpec(memory_space=pltpu.VMEM),
        scratch_shapes=[
            pltpu.VMEM((time_count, members, block, frames_dev), bf16),
            pltpu.VMEM(table.shape, bf16),
            pltpu.VMEM((nfreq * members, block), f32),
            pltpu.VMEM((nfreq * members, block), f32),
            pltpu.VMEM((2, 4, 16, half, width), f32),
            pltpu.VMEM((2, 16, 4, half, width), f32),
            pltpu.VMEM((4, 16, half, width), f32),
            pltpu.VMEM((16, 4, half, width), f32),
            pltpu.VMEM((4, 16, half, width), f32),
            pltpu.VMEM((16, half, width), f32),
            pltpu.VMEM((16, 4, half, width), f32),
            pltpu.VMEM((4, half, width), f32),
            dma, dma, dma((CHUNKS, 7)), dma((CHUNKS, 7)), dma((2,)), dma((2,)),
            dma((2, 4)), dma((2, 4)), dma((2, 16)), dma((2, 16)),
        ],
        compiler_params=pltpu.CompilerParams(collective_id=0, has_side_effects=True, vmem_limit_bytes=56 << 20),
    )(series, jnp.asarray(table))


def solution(mesh):
    placed = (P(None, "space", "tm"),)
    return jax.shard_map(
        shards, mesh=mesh, in_specs=placed, out_specs=P(("space", "tm"), None), check_vma=False
    )
```

time: 639 us -> 159 us (0.25)
  waiting for transfers between devices: 269 us -> 0 us
  matrix products: 199 us -> 0 us
  Pallas kernels: 0 us -> 156 us
  local copies, waits for them, and re-layouts: 94.6 us -> 1.38 us
  other arithmetic: 49.2 us -> 0 us
  between operations: 13.7 us -> 0.01 us
    dot_general x2 -> x0, matrix products: 199 us -> none  [the longest x1 111 us: shards(): jnp.einsum('mpt,jt->mpj', fluctuation, full_table, precision=lax.Precisio...]
    unnamed x2 -> x0, waiting for transfers between devices: 186 us -> none
    pallas_call x0 -> x1, Pallas kernels: none -> 156 us  [shards(): pl.pallas_call(functools.partial(kernel, norm), out_shape=jax.ShapeDtypeS...]
    all_to_all x1 -> x0, waiting for transfers between devices: 83.4 us -> none  [shards(): lax.all_to_all(series, 'tm', split_axis=1, concat_axis=2, tiled=True)]
    dot_general x2 -> x0, local copies, waits for them, and re-layouts: 40.5 us -> none  [shards(): jnp.einsum('mpt,jt->mpj', fluctuation, full_table, precision=lax.Precisio...]
    add x1 -> x0, other arithmetic: 19 us -> none  [cross_terms(): real_sum = gram_all[:, 0, 0] + gram_all[:, 1, 1]]
    mul x1 -> x0, local copies, waits for them, and re-layouts: 17.5 us -> none  [shards(): fluctuation = (values - time_mean) * window]
    mul x2 -> x0, other arithmetic: 14.8 us -> none  [the longest x1 10.5 us: shards(): fluctuation = (values - time_mean) * window]
  transfers between devices with their start and end apart: 2 -> 0, of which waited for: 2 -> 0; matrix products, arithmetic and copies ran while one was open for 2% -> 0% of each run, Pallas kernels for 0% -> 0%
where the time goes in v1:
time: 159 us; the launch traced here: 157 us
  Pallas kernels  156 us (98%)
    pallas_call x1, Pallas kernels, shards(): pl.pallas_call(functools.partial(kernel, norm), out_shape=jax.ShapeDtypeS...  156 us

profile of v1, /device:TPU:32, one launch (start us, length us, event | category | flops | bytes accessed | tf_op | source)
XLA Modules:
  0.0 157.1 jit_solution(15912980369643333036)
XLA Ops:
  0.0 155.7 %shard_map.28 = f32[4,2048]{1,0:T(4,128)} custom-call(bf16[32,1024,128]{2,1,0:T(8,128)(2,1)} %x_ref.1, bf16[4,2,256,1024]{3,2,1,0:T(8,128)(2,1)} %constant.2.clone.table_ref), custom_call_target="tpu_custom_call" | custom-call | tf_op jit(solution)/shard_map/pallas_call | solution.py:283
  155.7 1.4 copy.4

commit v2 on v1

--- a/solution.py
+++ b/solution.py
@@ -51,7 +51,7 @@
 
 def kernel(
     norm, x_ref, table_ref, o_ref,
-    recv, table, xre, xim, part_z, part_p, core_z, core_p, got_z, got_zp, got_p, got_pz,
+    recv, table, xre, xim, part, got_core, got_z, got_zp, got_p, got_pz,
     local_sem, table_sem, a2a_send, a2a_recv, core_send, core_recv, z_send, z_recv, p_send, p_recv,
 ):
     space, tm = lax.axis_index("space"), lax.axis_index("tm")
@@ -138,55 +138,33 @@
             out = jnp.where(lane_f == f, tile[f * members : (f + 1) * members], out)
         return out
 
-    def cross(zz, pp, cc):
-        sp, t = device(zz, pp, cc)
-        rows = pl.ds((sp * 8 + t) * (4 * members), 4 * members)
+    def cross(zz, yy, t, cc):
+        width = 4 * members
+        rows = pl.ds((zz * 32 + yy * 16 + cc * 8 + t) * width, width)
         re_hi, re_lo = split(xre[rows, :])
         im_hi, im_lo = split(xim[rows, :])
         a_hi = jnp.concatenate([re_hi, im_hi], axis=1)
         a_lo = jnp.concatenate([re_lo, im_lo], axis=1)
         b_hi = jnp.concatenate([a_hi, jnp.concatenate([-im_hi, re_hi], axis=1)], axis=0)
         b_lo = jnp.concatenate([a_lo, jnp.concatenate([-im_lo, re_lo], axis=1)], axis=0)
-        gram = matmul_nt(a_hi, b_hi) + matmul_nt(a_lo, b_hi) + matmul_nt(a_hi, b_lo)
-        return jnp.where(row >= lane_j, pick(gram[:, : 4 * members]), pick(gram[:, 4 * members :]))
-
-    other = 1 - core
-
-    @pl.loop(0, 64)
-    def _(n):
-        zz, pp = n // 16, n % 16
-        tile = cross(zz, pp, other)
-        part_z[0, zz, pp] = tile[:half]
-        part_p[0, pp, zz] = tile[half:]
-
-    def to_core(k):
+        both = matmul_nt(jnp.concatenate([a_hi, a_lo], axis=0), b_hi)
+        gram = both[:width] + both[width:] + matmul_nt(a_hi, b_lo)
+        return jnp.where(row >= lane_j, pick(gram[:, :width]), pick(gram[:, width:]))
+
+    def to_core(n):
+        zz = (z + 1 + n) % 4
         return pltpu.make_async_remote_copy(
-            src_ref=(part_z, part_p)[k].at[0],
-            dst_ref=(core_z, core_p)[k],
-            send_sem=core_send.at[k],
-            recv_sem=core_recv.at[k],
+            src_ref=part.at[0, zz],
+            dst_ref=got_core.at[zz],
+            send_sem=core_send.at[n],
+            recv_sem=core_recv.at[n],
             device_id=(space + 1 - 2 * core, tm),
             device_id_type=MESH,
         )
 
-    for k in range(2):
-        to_core(k).start()
-
-    @pl.loop(0, 64)
-    def _(n):
-        zz, pp = n // 16, n % 16
-        tile = cross(zz, pp, core)
-        part_z[1, zz, pp] = tile[:half]
-        part_p[1, pp, zz] = tile[half:]
-
-    for k in range(2):
-        to_core(k).wait_recv()
-    part_z[1] += core_z[...]
-    part_p[1] += core_p[...]
-
     def over_z(stage, d):
         zz = (z + d) % 4
-        src, dst = ((part_z.at[1, zz], got_z.at[d]), (part_p.at[1, plane, zz], got_pz.at[d]))[stage]
+        src, dst = ((part.at[1, zz, 0], got_z.at[d]), (part.at[1, zz, 1, plane], got_pz.at[d]))[stage]
         return pltpu.make_async_remote_copy(
             src_ref=src,
             dst_ref=dst,
@@ -196,48 +174,78 @@
             device_id_type=MESH,
         )
 
-    def over_plane(stage, d):
-        pp = plane_peer(d)
-        src, dst = ((part_p.at[1, pp], got_p.at[d]), (part_z.at[1, z, pp], got_zp.at[d]))[stage]
+    def over_plane(n, d):
+        pp, zz = plane_peer(d), (z + 1 + n) % 4
+        src, dst = (part.at[1, zz, 1, pp], got_p.at[zz, d])
+        if isinstance(n, int) and n == 4:
+            src, dst = part.at[1, z, 0, pp], got_zp.at[d]
         return pltpu.make_async_remote_copy(
             src_ref=src,
             dst_ref=dst,
-            send_sem=p_send.at[stage, d],
-            recv_sem=p_recv.at[stage, d],
+            send_sem=p_send.at[n, d],
+            recv_sem=p_recv.at[n, d],
             device_id=device(z, pp, core),
             device_id_type=MESH,
         )
 
-    for d in range(1, 4):
-        over_z(0, d).start()
-    for d in range(1, 16):
-        over_plane(0, d).start()
+    @pl.loop(0, 4)
+    def _(n):
+        zz = (z + 1 + n) % 4
+
+        @pl.loop(0, 2)
+        def _(yy):
+            for t in range(8):
+                tile = cross(zz, yy, t, 1 - core)
+                part[0, zz, 0, yy * 8 + t] = tile[:half]
+                part[0, zz, 1, yy * 8 + t] = tile[half:]
+
+        to_core(n).start()
+
+    @pl.loop(0, 4)
+    def _(n):
+        zz = (z + 1 + n) % 4
+        to_core(n).wait_recv()
+
+        @pl.loop(0, 2)
+        def _(yy):
+            for t in range(8):
+                tile = cross(zz, yy, t, core)
+                pp = yy * 8 + t
+                part[1, zz, 0, pp] = tile[:half] + got_core[zz, 0, pp]
+                part[1, zz, 1, pp] = tile[half:] + got_core[zz, 1, pp]
+
+        @pl.when(n < 3)
+        def _():
+            over_z(0, n + 1).start()
+
+        for d in range(1, 16):
+            over_plane(n, d).start()
+
+    def lower_sum(n):
+        zz = (z + 1 + n) % 4
+        for d in range(1, 16):
+            over_plane(n, d).wait_recv()
+        total = part[1, zz, 1, plane]
+        for d in range(1, 16):
+            total = total + got_p[zz, d]
+        return total
+
+    for n in range(3):
+        part[1, (z + 1 + n) % 4, 1, plane] = lower_sum(n)
+        over_z(1, n + 1).start()
     for d in range(1, 4):
         over_z(0, d).wait_recv()
-    total = part_z[1, z]
-    for d in range(1, 4):
-        total = total + got_z[d]
-    part_z[1, z] = total
+    part[1, z, 0] += got_z[1] + got_z[2] + got_z[3]
     for d in range(1, 16):
-        over_plane(1, d).start()
-    for d in range(1, 16):
-        over_plane(0, d).wait_recv()
-    total = part_p[1, plane]
-    for d in range(1, 16):
-        total = total + got_p[d]
-    part_p[1, plane] = total
-    for d in range(1, 4):
-        over_z(1, d).start()
-    for d in range(1, 16):
-        over_plane(1, d).wait_recv()
-    upper = part_z[1, z, plane]
-    for d in range(1, 16):
-        upper = upper + got_zp[d]
+        over_plane(4, d).start()
+    lower = lower_sum(3)
     for d in range(1, 4):
         over_z(1, d).wait_recv()
-    lower = part_p[1, plane, z]
-    for d in range(1, 4):
         lower = lower + got_pz[d]
+    upper = part[1, z, 0, plane]
+    for d in range(1, 16):
+        over_plane(4, d).wait_recv()
+        upper = upper + got_zp[d]
 
     mixed = jnp.concatenate([upper, lower], axis=0) * norm
     spread = jnp.concatenate([jnp.where(lane_f == f, mixed, 0.0) for f in range(4)], axis=0).T
@@ -246,14 +254,14 @@
         turned = turned + spread[f * members : (f + 1) * members]
     real = jnp.where(row >= lane_j, mixed, turned)
     imag = jnp.where(row < lane_j, mixed, jnp.where(row == lane_j, 0.0, -turned))
-    for part, value in enumerate((real, imag)):
+    for which, value in enumerate((real, imag)):
         for bit in (2, 1):
             row_bit, lane_bit = row // bit % 2, lane_f // bit % 2
             up = pltpu.roll(pltpu.roll(value, bit * members, 1), members - bit, 0)
             down = pltpu.roll(pltpu.roll(value, (4 - bit) * members, 1), bit, 0)
             value = jnp.where(row_bit == lane_bit, value, jnp.where(row_bit == 0, up, down))
         for u in range(members // 4):
-            start = (part * members // 4 + u) * 4 * members
+            start = (which * members // 4 + u) * 4 * members
             o_ref[:, start : start + 4 * members] = value[4 * u : 4 * u + 4]
 
     @pl.loop(0, CHUNKS)
@@ -261,13 +269,14 @@
         for r in range(len(TM_PEERS)):
             snapshots(c, r).wait_send()
 
-    for k in range(2):
-        to_core(k).wait_send()
-    for stage in range(2):
-        for d in range(1, 4):
-            over_z(stage, d).wait_send()
+    for n in range(4):
+        to_core(n).wait_send()
+    for d in range(1, 4):
+        over_z(0, d).wait_send()
+        over_z(1, d).wait_send()
+    for n in range(5):
         for d in range(1, 16):
-            over_plane(stage, d).wait_send()
+            over_plane(n, d).wait_send()
 
 
 def shards(series):
@@ -290,16 +299,14 @@
             pltpu.VMEM(table.shape, bf16),
             pltpu.VMEM((nfreq * members, block), f32),
             pltpu.VMEM((nfreq * members, block), f32),
-            pltpu.VMEM((2, 4, 16, half, width), f32),
-            pltpu.VMEM((2, 16, 4, half, width), f32),
-            pltpu.VMEM((4, 16, half, width), f32),
-            pltpu.VMEM((16, 4, half, width), f32),
+            pltpu.VMEM((2, 4, 2, 16, half, width), f32),
+            pltpu.VMEM((4, 2, 16, half, width), f32),
             pltpu.VMEM((4, 16, half, width), f32),
             pltpu.VMEM((16, half, width), f32),
-            pltpu.VMEM((16, 4, half, width), f32),
+            pltpu.VMEM((4, 16, half, width), f32),
             pltpu.VMEM((4, half, width), f32),
-            dma, dma, dma((CHUNKS, 7)), dma((CHUNKS, 7)), dma((2,)), dma((2,)),
-            dma((2, 4)), dma((2, 4)), dma((2, 16)), dma((2, 16)),
+            dma, dma, dma((CHUNKS, 7)), dma((CHUNKS, 7)), dma((4,)), dma((4,)),
+            dma((2, 4)), dma((2, 4)), dma((5, 16)), dma((5, 16)),
         ],
         compiler_params=pltpu.CompilerParams(collective_id=0, has_side_effects=True, vmem_limit_bytes=56 << 20),
     )(series, jnp.asarray(table))

time: 159 us -> 131 us (0.82); the launches traced: 157 us -> 131 us
  Pallas kernels: 156 us -> 129 us
    pallas_call x1, Pallas kernels: 156 us -> 129 us  [shards(): pl.pallas_call(functools.partial(kernel, norm), out_shape=jax.ShapeDtypeS...]
where the time goes in v2:
time: 131 us
  Pallas kernels  129 us (98%)
  local copies, waits for them, and re-layouts  1.38 us (1%)
    pallas_call x1, Pallas kernels, shards(): pl.pallas_call(functools.partial(kernel, norm), out_shape=jax.ShapeDtypeS...  129 us

profile of v2, /device:TPU:32, one launch (start us, length us, event | category | flops | bytes accessed | tf_op | source)
XLA Modules:
  0.0 130.9 jit_solution(12157219014777132869)
XLA Ops:
  0.0 129.5 %shard_map.28 = f32[4,2048]{1,0:T(4,128)} custom-call(bf16[32,1024,128]{2,1,0:T(8,128)(2,1)} %x_ref.1, bf16[4,2,256,1024]{3,2,1,0:T(8,128)(2,1)} %constant.2.clone.table_ref), custom_call_target="tpu_custom_call" | custom-call | tf_op jit(solution)/shard_map/pallas_call | solution.py:292
  129.5 1.4 %copy.4 = f32[4,2048]{1,0:T(4,128)} copy(f32[4,2048]{1,0:T(4,128)} %shard_map.28) | data formatting | bytes 65536

commit v3 on v2

--- a/solution.py
+++ b/solution.py
@@ -49,6 +49,10 @@
     return lax.dot_general(a, b, NT_DIMS, preferred_element_type=jnp.float32)
 
 
+def matmul(a, b):
+    return jnp.dot(a, b, preferred_element_type=jnp.float32)
+
+
 def kernel(
     norm, x_ref, table_ref, o_ref,
     recv, table, xre, xim, part, got_core, got_z, got_zp, got_p, got_pz,
@@ -143,12 +147,18 @@
         rows = pl.ds((zz * 32 + yy * 16 + cc * 8 + t) * width, width)
         re_hi, re_lo = split(xre[rows, :])
         im_hi, im_lo = split(xim[rows, :])
-        a_hi = jnp.concatenate([re_hi, im_hi], axis=1)
-        a_lo = jnp.concatenate([re_lo, im_lo], axis=1)
-        b_hi = jnp.concatenate([a_hi, jnp.concatenate([-im_hi, re_hi], axis=1)], axis=0)
-        b_lo = jnp.concatenate([a_lo, jnp.concatenate([-im_lo, re_lo], axis=1)], axis=0)
-        both = matmul_nt(jnp.concatenate([a_hi, a_lo], axis=0), b_hi)
-        gram = both[:width] + both[width:] + matmul_nt(a_hi, b_lo)
+        left = jnp.concatenate(
+            [jnp.concatenate([re_hi, im_hi], axis=1), jnp.concatenate([re_lo, im_lo], axis=1)], axis=0
+        )
+
+        def right(re, im):
+            re, im = re.T, im.T
+            return jnp.concatenate(
+                [jnp.concatenate([re, im], axis=0), jnp.concatenate([-im, re], axis=0)], axis=1
+            )
+
+        both = matmul(left, right(re_hi, im_hi))
+        gram = both[:width] + both[width:] + matmul(left[:width], right(re_lo, im_lo))
         return jnp.where(row >= lane_j, pick(gram[:, :width]), pick(gram[:, width:]))
 
     def to_core(n):
@@ -192,12 +202,10 @@
     def _(n):
         zz = (z + 1 + n) % 4
 
-        @pl.loop(0, 2)
-        def _(yy):
-            for t in range(8):
-                tile = cross(zz, yy, t, 1 - core)
-                part[0, zz, 0, yy * 8 + t] = tile[:half]
-                part[0, zz, 1, yy * 8 + t] = tile[half:]
+        for pp in range(16):
+            tile = cross(zz, pp // 8, pp % 8, 1 - core)
+            part[0, zz, 0, pp] = tile[:half]
+            part[0, zz, 1, pp] = tile[half:]
 
         to_core(n).start()
 
@@ -206,13 +214,10 @@
         zz = (z + 1 + n) % 4
         to_core(n).wait_recv()
 
-        @pl.loop(0, 2)
-        def _(yy):
-            for t in range(8):
-                tile = cross(zz, yy, t, core)
-                pp = yy * 8 + t
-                part[1, zz, 0, pp] = tile[:half] + got_core[zz, 0, pp]
-                part[1, zz, 1, pp] = tile[half:] + got_core[zz, 1, pp]
+        for pp in range(16):
+            tile = cross(zz, pp // 8, pp % 8, core)
+            part[1, zz, 0, pp] = tile[:half] + got_core[zz, 0, pp]
+            part[1, zz, 1, pp] = tile[half:] + got_core[zz, 1, pp]
 
         @pl.when(n < 3)
         def _():

time: 131 us -> 128 us (0.977)
  Pallas kernels: 129 us -> 127 us
    pallas_call x1, Pallas kernels: 129 us -> 127 us  [shards(): pl.pallas_call(functools.partial(kernel, norm), out_shape=jax.ShapeDtypeS...]
where the time goes in v3:
time: 128 us
  Pallas kernels  127 us (99%)
  local copies, waits for them, and re-layouts  1.38 us (1%)
    pallas_call x1, Pallas kernels, shards(): pl.pallas_call(functools.partial(kernel, norm), out_shape=jax.ShapeDtypeS...  127 us

profile of v3, /device:TPU:32, one launch (start us, length us, event | category | flops | bytes accessed | tf_op | source)
XLA Modules:
  0.0 128.0 jit_solution(11997598800815295039)
XLA Ops:
  0.0 126.6 %shard_map.28 = f32[4,2048]{1,0:T(4,128)} custom-call(bf16[32,1024,128]{2,1,0:T(8,128)(2,1)} %x_ref.1, bf16[4,2,256,1024]{3,2,1,0:T(8,128)(2,1)} %constant.2.clone.table_ref), custom_call_target="tpu_custom_call" | custom-call | tf_op jit(solution)/shard_map/pallas_call | solution.py:297
  126.6 1.4 %copy.4 = f32[4,2048]{1,0:T(4,128)} copy(f32[4,2048]{1,0:T(4,128)} %shard_map.28) | data formatting | bytes 65536

commit v4 on v3

--- a/solution.py
+++ b/solution.py
@@ -12,7 +12,8 @@
 
 MESH = pl.DeviceIdType.MESH
 NT_DIMS = (((1,), (1,)), ((), ()))
-CHUNKS = 8
+CHUNKS = 16
+GROUPS = 2
 FBLOCK = 128
 TM_PEERS = ((1, 0), (2, 1), (3, 0), (0, 1), (1, 1), (2, 0), (3, 1))
 
@@ -162,10 +163,9 @@
         return jnp.where(row >= lane_j, pick(gram[:, :width]), pick(gram[:, width:]))
 
     def to_core(n):
-        zz = (z + 1 + n) % 4
         return pltpu.make_async_remote_copy(
-            src_ref=part.at[0, zz],
-            dst_ref=got_core.at[zz],
+            src_ref=part.at[0, n],
+            dst_ref=got_core.at[n],
             send_sem=core_send.at[n],
             recv_sem=core_recv.at[n],
             device_id=(space + 1 - 2 * core, tm),
@@ -174,7 +174,7 @@
 
     def over_z(stage, d):
         zz = (z + d) % 4
-        src, dst = ((part.at[1, zz, 0], got_z.at[d]), (part.at[1, zz, 1, plane], got_pz.at[d]))[stage]
+        src, dst = ((part.at[1, d - 1, 0], got_z.at[d]), (part.at[1, d - 1, 1, plane], got_pz.at[d]))[stage]
         return pltpu.make_async_remote_copy(
             src_ref=src,
             dst_ref=dst,
@@ -184,72 +184,76 @@
             device_id_type=MESH,
         )
 
-    def over_plane(n, d):
-        pp, zz = plane_peer(d), (z + 1 + n) % 4
-        src, dst = (part.at[1, zz, 1, pp], got_p.at[zz, d])
-        if isinstance(n, int) and n == 4:
-            src, dst = part.at[1, z, 0, pp], got_zp.at[d]
+    def over_plane(k, d):
+        pp = plane_peer(d)
+        if isinstance(k, int) and k == GROUPS:
+            src, dst = part.at[1, 3, 0, pp], got_zp.at[d]
+        else:
+            some = pl.ds(k * (4 // GROUPS), 4 // GROUPS)
+            src, dst = part.at[1, some, 1, pp], got_p.at[some, d]
         return pltpu.make_async_remote_copy(
             src_ref=src,
             dst_ref=dst,
-            send_sem=p_send.at[n, d],
-            recv_sem=p_recv.at[n, d],
+            send_sem=p_send.at[k, d],
+            recv_sem=p_recv.at[k, d],
             device_id=device(z, pp, core),
             device_id_type=MESH,
         )
 
-    @pl.loop(0, 4)
-    def _(n):
-        zz = (z + 1 + n) % 4
-
-        for pp in range(16):
-            tile = cross(zz, pp // 8, pp % 8, 1 - core)
-            part[0, zz, 0, pp] = tile[:half]
-            part[0, zz, 1, pp] = tile[half:]
-
-        to_core(n).start()
-
-    @pl.loop(0, 4)
-    def _(n):
-        zz = (z + 1 + n) % 4
-        to_core(n).wait_recv()
-
-        for pp in range(16):
-            tile = cross(zz, pp // 8, pp % 8, core)
-            part[1, zz, 0, pp] = tile[:half] + got_core[zz, 0, pp]
-            part[1, zz, 1, pp] = tile[half:] + got_core[zz, 1, pp]
-
-        @pl.when(n < 3)
+    @pl.loop(0, 5)
+    def _(step):
+        @pl.when(step < 4)
         def _():
-            over_z(0, n + 1).start()
-
+            zz = (z + 1 + step) % 4
+            for pp in range(16):
+                tile = cross(zz, pp // 8, pp % 8, 1 - core)
+                part[0, step, 0, pp] = tile[:half]
+                part[0, step, 1, pp] = tile[half:]
+            to_core(step).start()
+
+        @pl.when(step > 0)
+        def _():
+            n = step - 1
+            zz = (z + 1 + n) % 4
+            to_core(n).wait_recv()
+            for pp in range(16):
+                tile = cross(zz, pp // 8, pp % 8, core)
+                part[1, n, 0, pp] = tile[:half] + got_core[n, 0, pp]
+                part[1, n, 1, pp] = tile[half:] + got_core[n, 1, pp]
+
+            @pl.when(n < 3)
+            def _():
+                over_z(0, n + 1).start()
+
+            @pl.when(step % (4 // GROUPS) == 0)
+            def _():
+                for d in range(1, 16):
+                    over_plane(n // (4 // GROUPS), d).start()
+
+    def lower_sum(n):
+        if n % (4 // GROUPS) == 0:
+            for d in range(1, 16):
+                over_plane(n // (4 // GROUPS), d).wait_recv()
+        total = part[1, n, 1, plane]
         for d in range(1, 16):
-            over_plane(n, d).start()
-
-    def lower_sum(n):
-        zz = (z + 1 + n) % 4
-        for d in range(1, 16):
-            over_plane(n, d).wait_recv()
-        total = part[1, zz, 1, plane]
-        for d in range(1, 16):
-            total = total + got_p[zz, d]
+            total = total + got_p[n, d]
         return total
 
     for n in range(3):
-        part[1, (z + 1 + n) % 4, 1, plane] = lower_sum(n)
+        part[1, n, 1, plane] = lower_sum(n)
         over_z(1, n + 1).start()
     for d in range(1, 4):
         over_z(0, d).wait_recv()
-    part[1, z, 0] += got_z[1] + got_z[2] + got_z[3]
+    part[1, 3, 0] += got_z[1] + got_z[2] + got_z[3]
     for d in range(1, 16):
-        over_plane(4, d).start()
+        over_plane(GROUPS, d).start()
     lower = lower_sum(3)
     for d in range(1, 4):
         over_z(1, d).wait_recv()
         lower = lower + got_pz[d]
-    upper = part[1, z, 0, plane]
+    upper = part[1, 3, 0, plane]
     for d in range(1, 16):
-        over_plane(4, d).wait_recv()
+        over_plane(GROUPS, d).wait_recv()
         upper = upper + got_zp[d]
 
     mixed = jnp.concatenate([upper, lower], axis=0) * norm
@@ -279,9 +283,9 @@
     for d in range(1, 4):
         over_z(0, d).wait_send()
         over_z(1, d).wait_send()
-    for n in range(5):
+    for k in range(GROUPS + 1):
         for d in range(1, 16):
-            over_plane(n, d).wait_send()
+            over_plane(k, d).wait_send()
 
 
 def shards(series):
@@ -311,7 +315,7 @@
             pltpu.VMEM((4, 16, half, width), f32),
             pltpu.VMEM((4, half, width), f32),
             dma, dma, dma((CHUNKS, 7)), dma((CHUNKS, 7)), dma((4,)), dma((4,)),
-            dma((2, 4)), dma((2, 4)), dma((5, 16)), dma((5, 16)),
+            dma((2, 4)), dma((2, 4)), dma((GROUPS + 1, 16)), dma((GROUPS + 1, 16)),
         ],
         compiler_params=pltpu.CompilerParams(collective_id=0, has_side_effects=True, vmem_limit_bytes=56 << 20),
     )(series, jnp.asarray(table))

time: 128 us -> 128 us (level)
  no operation moved by 1% of the time
where the time goes in v4:
time: 128 us; the launch traced here: 127 us
  Pallas kernels  126 us (98%)
  local copies, waits for them, and re-layouts  1.38 us (1%)
    pallas_call x1, Pallas kernels, shards(): pl.pallas_call(functools.partial(kernel, norm), out_shape=jax.ShapeDtypeS...  126 us

profile of v4, /device:TPU:32, one launch (start us, length us, event | category | flops | bytes accessed | tf_op | source)
XLA Modules:
  0.0 126.9 jit_solution(10093251193331532157)
XLA Ops:
  0.0 125.5 %shard_map.28 = f32[4,2048]{1,0:T(4,128)} custom-call(bf16[32,1024,128]{2,1,0:T(8,128)(2,1)} %x_ref.1, bf16[4,2,256,1024]{3,2,1,0:T(8,128)(2,1)} %constant.2.clone.table_ref), custom_call_target="tpu_custom_call" | custom-call | tf_op jit(solution)/shard_map/pallas_call | solution.py:301
  125.5 1.4 %copy.4 = f32[4,2048]{1,0:T(4,128)} copy(f32[4,2048]{1,0:T(4,128)} %shard_map.28) | data formatting | bytes 65536

commit v5 on v4

--- a/solution.py
+++ b/solution.py
@@ -239,14 +239,18 @@
             total = total + got_p[n, d]
         return total
 
-    for n in range(3):
+    def pass_lower(n):
         part[1, n, 1, plane] = lower_sum(n)
         over_z(1, n + 1).start()
+
+    for n in range(2):
+        pass_lower(n)
     for d in range(1, 4):
         over_z(0, d).wait_recv()
     part[1, 3, 0] += got_z[1] + got_z[2] + got_z[3]
     for d in range(1, 16):
         over_plane(GROUPS, d).start()
+    pass_lower(2)
     lower = lower_sum(3)
     for d in range(1, 4):
         over_z(1, d).wait_recv()

time: 128 us -> 126 us (0.984); the launches traced: 127 us -> 126 us
  no operation moved by 1% of the time
where the time goes in v5:
time: 126 us
  Pallas kernels  125 us (99%)
  local copies, waits for them, and re-layouts  1.38 us (1%)
    pallas_call x1, Pallas kernels, shards(): pl.pallas_call(functools.partial(kernel, norm), out_shape=jax.ShapeDtypeS...  125 us

profile of v5, /device:TPU:32, one launch (start us, length us, event | category | flops | bytes accessed | tf_op | source)
XLA Modules:
  0.0 126.3 jit_solution(9277511419752665932)
XLA Ops:
  0.0 124.9 %shard_map.28 = f32[4,2048]{1,0:T(4,128)} custom-call(bf16[32,1024,128]{2,1,0:T(8,128)(2,1)} %x_ref.1, bf16[4,2,256,1024]{3,2,1,0:T(8,128)(2,1)} %constant.2.clone.table_ref), custom_call_target="tpu_custom_call" | custom-call | tf_op jit(solution)/shard_map/pallas_call | solution.py:305
  124.9 1.4 %copy.4 = f32[4,2048]{1,0:T(4,128)} copy(f32[4,2048]{1,0:T(4,128)} %shard_map.28) | data formatting | bytes 65536

commit v6 on v5

--- a/solution.py
+++ b/solution.py
@@ -13,7 +13,7 @@
 MESH = pl.DeviceIdType.MESH
 NT_DIMS = (((1,), (1,)), ((), ()))
 CHUNKS = 16
-GROUPS = 2
+GROUPS = 4
 FBLOCK = 128
 TM_PEERS = ((1, 0), (2, 1), (3, 0), (0, 1), (1, 1), (2, 0), (3, 1))
 

time: 126 us -> 127 us (level)
  no operation moved by 1% of the time
where the time goes in v6:
time: 127 us
  Pallas kernels  126 us (99%)
  local copies, waits for them, and re-layouts  1.38 us (1%)
    pallas_call x1, Pallas kernels, shards(): pl.pallas_call(functools.partial(kernel, norm), out_shape=jax.ShapeDtypeS...  126 us

profile of v6, /device:TPU:32, one launch (start us, length us, event | category | flops | bytes accessed | tf_op | source)
XLA Modules:
  0.0 127.1 jit_solution(13671454459471855710)
XLA Ops:
  0.0 125.7 %shard_map.28 = f32[4,2048]{1,0:T(4,128)} custom-call(bf16[32,1024,128]{2,1,0:T(8,128)(2,1)} %x_ref.1, bf16[4,2,256,1024]{3,2,1,0:T(8,128)(2,1)} %constant.2.clone.table_ref), custom_call_target="tpu_custom_call" | custom-call | tf_op jit(solution)/shard_map/pallas_call | solution.py:305
  125.7 1.4 %copy.4 = f32[4,2048]{1,0:T(4,128)} copy(f32[4,2048]{1,0:T(4,128)} %shard_map.28) | data formatting | bytes 65536
